TPU v7x, 512 devices: a whole 4x4x16 slice. The times are simulated.
512 devices in a mesh: view: 8 (over y, x_lo), batch: 64 (over x_hi, z, core).
Axes of the slice: x: 4 (x_hi: 2, x_lo: 2; x = x_hi * 2 + x_lo), y: 4, z: 16, core: 2. Of those that a mesh axis runs over, the one named last changes fastest.
Arguments:
- embeddings: bfloat16 [8, 8192, 256], P('view', 'batch'), may hold values from -1.5 to 1.5
- positive: int32 [8, 8192], P(None, 'batch'), may hold values from 0 to 127, as said below
Outputs:
- gradients: float32 [8, 8192, 256], P('view', 'batch')
- totals: float32 [8, 8192], P('view', 'batch')
- row_loss: float32 [8, 8192], P('view', 'batch')
Inputs may be any that keep to these rules, and one draw needn't show every extreme that they name: `positive`: for each view and each aligned block of 128 samples, the entries are a permutation of 0 to 127.
All inputs are finite; a program needn't handle non-finite values.
Results may differ from a plain program's by a relative error of at most 0.002.
Values may be sent and summed in bfloat16 or wider, within the bound.
No kernel may reach another device: no remote copies, remote signals or barrier semaphores. Data moves between devices by JAX's collectives and lax.ppermute only.
A program may use at most 64 MiB of HBM per device.

v0:
```python
import jax
import jax.numpy as jnp
from jax import lax
from jax.sharding import PartitionSpec as P

logit_scale = 10.0


def from_partner(value, axis, bit):
    return lax.ppermute(value, axis, [(i, i ^ 1 << bit) for i in range(lax.axis_size(axis))])


def body(embeddings, positive):
    own_rows = embeddings[0]
    row_count = own_rows.shape[0]
    view_count = lax.axis_size("view")
    swap_bit = view_count.bit_length() - 2
    partner = from_partner(own_rows, "view", swap_bit)
    view_index = lax.axis_index("view")
    own_match = lax.dynamic_index_in_dim(positive, view_index, 0, keepdims=False)
    far_match = lax.dynamic_index_in_dim(
        positive, jnp.bitwise_xor(view_index, view_count // 2), 0, keepdims=False
    )

    def score_piece(key_piece):
        return (
            jnp.einsum("ie,je->ij", own_rows, key_piece, preferred_element_type=jnp.float32)
            * logit_scale
        )

    running_max = jnp.full((row_count,), -1e30, jnp.float32)
    scores = score_piece(lax.all_gather(partner, "batch", axis=0, tiled=True))
    new_max = jnp.maximum(running_max, jnp.max(scores, axis=1))
    summed = jnp.sum(jnp.exp(scores - new_max[:, None]), axis=1)
    running_max, summed = (new_max, summed)
    totals = running_max + jnp.log(summed)
    far_totals = from_partner(totals, "view", swap_bit)
    every_total = lax.all_gather(far_totals, "batch", axis=0, tiled=True)
    key_piece = lax.all_gather(partner, "batch", axis=0, tiled=True)
    scores = score_piece(key_piece)
    w_rows = jnp.exp(scores - totals[:, None]).astype(jnp.bfloat16)
    w_cols = jnp.exp(scores - every_total[None, :]).astype(jnp.bfloat16)
    products = jnp.dot(
        jnp.concatenate([w_rows, w_cols], axis=0), key_piece, preferred_element_type=jnp.float32
    )
    own_acc = products[:row_count]
    side_acc = products[row_count:]
    spread = own_acc + side_acc
    pos_rows = jnp.take(partner, own_match, axis=0).astype(jnp.float32)
    pos_score = jnp.sum(own_rows.astype(jnp.float32) * pos_rows, axis=1) * logit_scale
    row_loss = totals - pos_score
    row_ids = jnp.arange(row_count, dtype=jnp.int32)
    matched_hot = (far_match[None, :] == row_ids[:, None]).astype(jnp.bfloat16)
    matched = jnp.dot(matched_hot, partner, preferred_element_type=jnp.float32)
    gradients = logit_scale * (spread - pos_rows - matched)
    return (gradients[None], totals[None], row_loss[None])


def solution(mesh):
    return jax.shard_map(
        body,
        mesh=mesh,
        in_specs=(P("view", "batch", None), P(None, "batch")),
        out_specs=(P("view", "batch", None), P("view", "batch"), P("view", "batch")),
        check_vma=False,
    )
```

profile of v0, /device:TPU:1, one launch (start us, length us, event | category | flops | bytes accessed | tf_op | source)
XLA Modules:
  0.0 268.4 jit_solution(11104582229734057468)
XLA Ops:
  7.2 0.0 all-gather.3.cloned.1.call-start
  7.2 5.6 %collective-permute-start = (bf16[128,256]{1,0:T(8,128)(2,1)}, bf16[128,256]{1,0:T(8,128)(2,1)S(1)}, u32[]{:S(2)}, u32[]{:S(2)}) collective-permute-start(bf16[128,256]{1,0:T(8,128)(2,1)} %bitcast.25), channel_id=1, source_target_pairs={{0,256},{64,320},{128,384},{192,448},{256,0},{320,64},{384,128},{4... | collective-permute-start | bytes 196616 | tf_op jit(solution)/shard_map/ppermute | solution.py:10
  12.9 1.9 collective-permute-done
  14.7 0.0 copy-start
  14.7 0.6 copy-done
  15.3 0.0 all-gather.3.cloned.1.call-update
  15.4 0.7 fusion.10
  16.1 0.7 compare_and_fusion
  16.8 0.7 dynamic-slice_bitcast_fusion
  17.5 1.6 gather_fusion
  19.1 1.0 fusion.7
  20.1 152.4 %all-gather.3.cloned.1.call-done = bf16[8192,256]{1,0:T(8,128)(2,1)} async-done(((bf16[128,256]{1,0:T(8,128)(2,1)}), bf16[8192,256]{1,0:T(8,128)(2,1)}) %all-gather.3.cloned.1.call-update) | async-done | bytes 4194320 | tf_op jit(solution)/shard_map/all_gather | solution.py:39
  172.5 3.8 %fusion.13 = (f32[128]{0:T(128)S(1)}, f32[128,8192]{1,0:T(8,128)S(1)}) fusion(bf16[8192,256]{1,0:T(8,128)(2,1)} %all-gather.3.cloned.1.call-done, bf16[1,128,256]{2,1,0:T(8,128)(2,1)} %param.2), kind=kOutput, calls=%fused_computation.32 | convolution fusion | flops 538967936 | bytes 8454656 | tf_op jit(solution)/shard_map/ie,je->ij/dot_general | solution.py:27
  176.3 0.8 exponential_reduce_fusion
  177.0 0.0 copy-start.3
  177.1 4.6 %collective-permute-start.1 = (f32[128]{0:T(128)S(1)}, f32[128]{0:T(128)S(1)}, u32[]{:S(2)}, u32[]{:S(2)}) collective-permute-start(f32[128]{0:T(128)S(1)} %log_add_fusion), channel_id=1, source_target_pairs={{0,256},{64,320},{128,384},{192,448},{256,0},{320,64},{384,128},{4... | collective-permute-start | bytes 1544 | tf_op jit(solution)/shard_map/ppermute | solution.py:10
  181.7 0.5 bitcast_subtract_fusion
  182.2 0.7 collective-permute-done.1
  182.9 74.4 %all-gather = f32[64,1,128]{2,1,0:T(1,128)S(1)} all-gather(f32[1,1,128]{2,1,0:T(1,128)S(1)} %bitcast.28), channel_id=1, replica_groups=mesh['view'=8,'batch'=64] {'batch'}, dimensions={0}, use_global_device_ids=true | all-gather | bytes 33280 | tf_op jit(solution)/shard_map/all_gather | solution.py:38
  257.3 0.0 copy-start.2
  257.3 1.5 exponential_convert_fusion.1
  258.7 0.0 copy-done.3
  258.8 0.7 copy-done.2
  259.5 0.0 copy-start.1
  259.5 1.2 fusion
  260.7 0.0 copy-done.1
  260.7 0.8 fusion.6
  (3 shorter events, 0.0 us)
Async XLA Ops:
  7.2 165.3 %all-gather.3.cloned.1.call-start = ((), (), s32[]{:S(2)}) async-start(), calls=%async_computation | async-start | bytes 4259840 | tf_op jit(solution)/shard_map/all_gather | solution.py:39
  7.2 7.5 %collective-permute-start = (bf16[128,256]{1,0:T(8,128)(2,1)}, bf16[128,256]{1,0:T(8,128)(2,1)S(1)}, u32[]{:S(2)}, u32[]{:S(2)}) collective-permute-start(bf16[128,256]{1,0:T(8,128)(2,1)} %bitcast.25), channel_id=1, source_target_pairs={{0,256},{64,320},{128,384},{192,448},{256,0},{320,64},{384,128},{4... | collective-permute-start | bytes 196616 | tf_op jit(solution)/shard_map/ppermute | solution.py:10
  14.7 0.6 copy-start
  177.0 81.7 %copy-start.3 = (f32[128]{0:T(128)}, f32[128]{0:T(128)S(1)}, u32[]{:S(2)}) copy-start(f32[128]{0:T(128)S(1)} %log_add_fusion) | copy-start | bytes 1540
  177.1 5.8 %collective-permute-start.1 = (f32[128]{0:T(128)S(1)}, f32[128]{0:T(128)S(1)}, u32[]{:S(2)}, u32[]{:S(2)}) collective-permute-start(f32[128]{0:T(128)S(1)} %log_add_fusion), channel_id=1, source_target_pairs={{0,256},{64,320},{128,384},{192,448},{256,0},{320,64},{384,128},{4... | collective-permute-start | bytes 1544 | tf_op jit(solution)/shard_map/ppermute | solution.py:10
  257.3 2.2 copy-start.2
  259.5 1.3 copy-start.1
Sparse Core Ops, SparseCore 0:
  15.5 156.9 all-gather.2
where the time goes:
time: 269 us; the launch traced here: 268 us
  waiting for transfers between devices  155 us (58%)
  blocking collectives  74.4 us (28%)
  between operations  14.1 us (5%)
  starting transfers between devices  10.3 us (4%)
  matrix products  5.86 us (2%)
  other arithmetic  5.15 us (2%)
  local copies, waits for them, and re-layouts  3.66 us (1%)
    all_gather x1, waiting for transfers between devices, body(): key_piece = lax.all_gather(partner, 'batch', axis=0, tiled=True)  152 us
    all_gather x1, blocking collectives, body(): every_total = lax.all_gather(far_totals, 'batch', axis=0, tiled=True)  74.4 us
    ppermute x2, starting transfers between devices, from_partner(): lax.ppermute(value, axis, [(i, i ^ 1 << bit) for i in range(lax.axis_size...  10.3 us
  transfers between devices with their start and end apart: 3, of which 3 were waited for; matrix products, arithmetic and copies ran while one was open for 2% of the time, Pallas kernels for 0%

commit v1 on v0

--- a/solution.py
+++ b/solution.py
@@ -35,7 +35,15 @@
     running_max, summed = (new_max, summed)
     totals = running_max + jnp.log(summed)
     far_totals = from_partner(totals, "view", swap_bit)
-    every_total = lax.all_gather(far_totals, "batch", axis=0, tiled=True)
+    every_total = jnp.concatenate(
+        lax.all_to_all(
+            jnp.stack([far_totals] * lax.axis_size("batch")),
+            axis_name="batch",
+            split_axis=0,
+            concat_axis=0,
+        ),
+        0,
+    )
     key_piece = lax.all_gather(partner, "batch", axis=0, tiled=True)
     scores = score_piece(key_piece)
     w_rows = jnp.exp(scores - totals[:, None]).astype(jnp.bfloat16)

time: 269 us -> 222 us (0.83)
  blocking collectives: 74.4 us -> 0 us
  waiting for transfers between devices: 155 us -> 170 us
  starting transfers between devices: 10.3 us -> 19.2 us
    all_gather x1 -> x0, blocking collectives: 74.4 us -> none  [body(): every_total = lax.all_gather(far_totals, 'batch', axis=0, tiled=True)]
    all_to_all x0 -> x1, waiting for transfers between devices: none -> 14.1 us  [body(): lax.all_to_all(jnp.stack([far_totals] * lax.axis_size('batch')), axis_nam...]
    all_to_all x0 -> x1, starting transfers between devices: none -> 8.9 us  [body(): lax.all_to_all(jnp.stack([far_totals] * lax.axis_size('batch')), axis_nam...]
  transfers between devices with their start and end apart: 3 -> 4, of which waited for: 3 -> 4; matrix products, arithmetic and copies ran while one was open for 2% -> 2% of each run, Pallas kernels for 0% -> 0%
where the time goes in v1:
time: 222 us; the launch traced here: 221 us
  waiting for transfers between devices  170 us (77%)
  starting transfers between devices  19.2 us (9%)
  between operations  14.2 us (6%)
  other arithmetic  6.3 us (3%)
  matrix products  5.86 us (3%)
  local copies, waits for them, and re-layouts  5.53 us (2%)
    all_gather x1, waiting for transfers between devices, body(): key_piece = lax.all_gather(partner, 'batch', axis=0, tiled=True)  153 us
    all_to_all x1, waiting for transfers between devices, body(): lax.all_to_all(jnp.stack([far_totals] * lax.axis_size('batch')), axis_nam...  14.1 us
    ppermute x2, starting transfers between devices, from_partner(): lax.ppermute(value, axis, [(i, i ^ 1 << bit) for i in range(lax.axis_size...  10.3 us
    all_to_all x1, starting transfers between devices, body(): lax.all_to_all(jnp.stack([far_totals] * lax.axis_size('batch')), axis_nam...  8.9 us
  transfers between devices with their start and end apart: 4, of which 4 were waited for; matrix products, arithmetic and copies ran while one was open for 2% of the time, Pallas kernels for 0%

profile of v1, /device:TPU:1, one launch (start us, length us, event | category | flops | bytes accessed | tf_op | source)
XLA Modules:
  0.0 221.4 jit_solution(7015144948123884055)
XLA Ops:
  7.2 0.0 all-gather.2.cloned.1.call-start
  7.2 5.6 %collective-permute-start = (bf16[128,256]{1,0:T(8,128)(2,1)}, bf16[128,256]{1,0:T(8,128)(2,1)S(1)}, u32[]{:S(2)}, u32[]{:S(2)}) collective-permute-start(bf16[128,256]{1,0:T(8,128)(2,1)} %bitcast.24), channel_id=1, source_target_pairs={{0,256},{64,320},{128,384},{192,448},{256,0},{320,64},{384,128},{4... | collective-permute-start | bytes 196616 | tf_op jit(solution)/shard_map/ppermute | solution.py:10
  12.9 1.9 collective-permute-done
  14.7 0.0 copy-start.1
  14.7 0.6 copy-done.1
  15.3 0.0 all-gather.2.cloned.1.call-update
  15.4 0.7 fusion.10
  16.1 0.7 compare_and_fusion
  16.8 0.7 dynamic-slice_bitcast_fusion
  17.5 1.6 gather_fusion
  19.1 153.4 %all-gather.2.cloned.1.call-done = bf16[8192,256]{1,0:T(8,128)(2,1)} async-done(((bf16[128,256]{1,0:T(8,128)(2,1)}), bf16[8192,256]{1,0:T(8,128)(2,1)}) %all-gather.2.cloned.1.call-update) | async-done | bytes 4194320 | tf_op jit(solution)/shard_map/all_gather | solution.py:47
  172.5 3.8 %fusion.13 = (f32[128]{0:T(128)S(1)}, f32[128,8192]{1,0:T(8,128)S(1)}) fusion(bf16[8192,256]{1,0:T(8,128)(2,1)} %all-gather.2.cloned.1.call-done, bf16[1,128,256]{2,1,0:T(8,128)(2,1)} %param.2), kind=kOutput, calls=%fused_computation.32 | convolution fusion | flops 538967936 | bytes 8454656 | tf_op jit(solution)/shard_map/ie,je->ij/dot_general | solution.py:27
  176.3 0.0 copy-start
  176.3 0.0 copy-start.4
  176.3 1.9 copy-done
  178.2 0.7 exponential_reduce_fusion
  179.0 0.0 copy-start.5
  179.0 4.6 %collective-permute-start.1 = (f32[128]{0:T(128)S(1)}, f32[128]{0:T(128)S(1)}, u32[]{:S(2)}, u32[]{:S(2)}) collective-permute-start(f32[128]{0:T(128)S(1)} %log_add_fusion), channel_id=1, source_target_pairs={{0,256},{64,320},{128,384},{192,448},{256,0},{320,64},{384,128},{4... | collective-permute-start | bytes 1544 | tf_op jit(solution)/shard_map/ppermute | solution.py:10
  183.7 0.0 copy-done.4
  183.7 0.2 fusion.7
  183.8 1.0 collective-permute-done.1
  184.8 0.6 stack.2
  185.5 8.9 %all-to-all-start = ((f32[64,1,128]{2,1,0:T(1,128)}), f32[64,1,128]{2,1,0:T(1,128)S(1)}, u32[]{:S(2)}, u32[]{:S(2)}) async-start(f32[64,1,128]{2,1,0:T(1,128)} %stack.2), calls=%async_computation | async-start | bytes 65536 | tf_op jit(solution)/shard_map/all_to_all | solution.py:39
  194.4 0.5 bitcast_subtract_fusion
  194.9 14.1 %all-to-all-done = f32[64,1,128]{2,1,0:T(1,128)S(1)} async-done(((f32[64,1,128]{2,1,0:T(1,128)}), f32[64,1,128]{2,1,0:T(1,128)S(1)}, u32[]{:S(2)}, u32[]{:S(2)}) %all-to-all-start) | async-done | bytes 32800 | tf_op jit(solution)/shard_map/all_to_all | solution.py:39
  209.0 0.0 copy-start.3
  209.0 3.5 %exponential_convert_fusion.1 = (bf16[128,8192]{1,0:T(8,128)(2,1)S(1)}, bf16[128,8192]{1,0:T(8,128)(2,1)S(1)}) fusion(f32[128,8192]{1,0:T(8,128)} %copy-done, f32[128]{0:T(128)S(1)} %log_add_fusion, f32[8192]{0:T(1024)S(1)} %bitcast.25), kind=kLoop, calls=%fused_computation.7 | loop fusion | flops 4194304 | bytes 8421888 | tf_op jit(solution)/shard_map/convert_element_type | solution.py:49
  212.5 0.0 copy-done.5
  212.5 0.0 copy-done.3
  212.5 0.0 copy-start.2
  212.5 1.2 fusion
  213.8 0.0 copy-done.2
  213.8 0.8 fusion.6
  (3 shorter events, 0.0 us)
Async XLA Ops:
  7.2 165.3 %all-gather.2.cloned.1.call-start = ((), (), s32[]{:S(2)}) async-start(), calls=%async_computation.1 | async-start | bytes 4259840 | tf_op jit(solution)/shard_map/all_gather | solution.py:47
  7.2 7.5 %collective-permute-start = (bf16[128,256]{1,0:T(8,128)(2,1)}, bf16[128,256]{1,0:T(8,128)(2,1)S(1)}, u32[]{:S(2)}, u32[]{:S(2)}) collective-permute-start(bf16[128,256]{1,0:T(8,128)(2,1)} %bitcast.24), channel_id=1, source_target_pairs={{0,256},{64,320},{128,384},{192,448},{256,0},{320,64},{384,128},{4... | collective-permute-start | bytes 196616 | tf_op jit(solution)/shard_map/ppermute | solution.py:10
  14.7 0.6 copy-start.1
  176.3 2.0 copy-start
  176.3 7.4 %copy-start.4 = (bf16[1,128,256]{2,1,0:T(8,128)(2,1)S(1)}, bf16[1,128,256]{2,1,0:T(8,128)(2,1)}, u32[]{:S(2)}) copy-start(bf16[1,128,256]{2,1,0:T(8,128)(2,1)} %param.2) | copy-start | bytes 196612
  179.0 33.5 %copy-start.5 = (f32[128]{0:T(128)}, f32[128]{0:T(128)S(1)}, u32[]{:S(2)}) copy-start(f32[128]{0:T(128)S(1)} %log_add_fusion) | copy-start | bytes 1540
  179.0 5.8 %collective-permute-start.1 = (f32[128]{0:T(128)S(1)}, f32[128]{0:T(128)S(1)}, u32[]{:S(2)}, u32[]{:S(2)}) collective-permute-start(f32[128]{0:T(128)S(1)} %log_add_fusion), channel_id=1, source_target_pairs={{0,256},{64,320},{128,384},{192,448},{256,0},{320,64},{384,128},{4... | collective-permute-start | bytes 1544 | tf_op jit(solution)/shard_map/ppermute | solution.py:10
  185.5 23.6 %all-to-all-start = ((f32[64,1,128]{2,1,0:T(1,128)}), f32[64,1,128]{2,1,0:T(1,128)S(1)}, u32[]{:S(2)}, u32[]{:S(2)}) async-start(f32[64,1,128]{2,1,0:T(1,128)} %stack.2), calls=%async_computation | async-start | bytes 65536 | tf_op jit(solution)/shard_map/all_to_all | solution.py:39
  209.0 3.5 %copy-start.3 = (bf16[8192,256]{1,0:T(8,128)(2,1)S(1)}, bf16[8192,256]{1,0:T(8,128)(2,1)}, u32[]{:S(2)}) copy-start(bf16[8192,256]{1,0:T(8,128)(2,1)} %all-gather.2.cloned.1.call-done) | copy-start | bytes 12582916
  212.5 1.3 copy-start.2
Sparse Core Ops, SparseCore 0:
  15.5 156.9 all-gather.1
